TPU v7x, 256 devices: a whole 4x4x8 slice. The times are simulated.
256 devices in a mesh: obs: 64 (over z, x, core), sub: 4 (over y).
Axes of the slice: x: 4, y: 4, z: 8, core: 2. Of those that a mesh axis runs over, the one named last changes fastest.
Arguments:
- jacobian: bfloat16 [262144, 2048], P(('obs', 'sub')), may hold values from -0.09375 to 0.09375
- obs_weight: float32 [262144], P(('obs', 'sub')), may hold values from 0.2 to 5
- row_counts: int32 [64], P('obs'), may hold values from 1 to 4096, 196608 in all
- tile_lists: int32 [64, 8], replicated, may hold values from 0 to 15, all different within a row
- tile_slot: int32 [16], replicated, may hold values from 0 to 15, each once
- probe_block: bfloat16 [4096, 256], P('obs'), may hold values from -6 to 6
Outputs:
- owned_product: bfloat16 [4096, 256], P('obs', 'sub')
Inputs may be any that keep to these rules, and one draw needn't show every extreme that they name: `row_counts`: the live counts of one block; some block is full (4096) in every draw. `tile_lists`: each row lists 8 different tiles; every tile is listed by some block. `tile_slot`: a permutation of the tiles.
All inputs are finite; a program needn't handle non-finite values.
Results may differ from a plain program's by a relative error of at most 0.0034.
Values may be sent and summed in bfloat16 or wider, within the bound.
A program may use at most 64 MiB of HBM per device.

v0:
```python
import jax
import jax.numpy as jnp
from jax import lax
from jax.sharding import PartitionSpec as P


def local(jacobian, obs_weight, row_counts, tile_lists, tile_slot, probe_block):
    rows = jacobian.shape[0]
    width = jacobian.shape[1]
    tiles_listed = tile_lists.shape[1]
    tile_count = tile_slot.shape[0]
    tile_rows = width // tiles_listed
    obs_count = lax.axis_size("obs")
    own_rows = tile_count * tile_rows // obs_count
    block_id = lax.axis_index("obs")
    sub_id = lax.axis_index("sub")
    offset = sub_id * rows
    live = (offset + jnp.arange(rows, dtype=jnp.int32) < row_counts[0]).astype(jnp.float32)
    weighted = (jacobian.astype(jnp.float32) * (obs_weight * live)[:, None]).astype(jnp.bfloat16)
    my_tiles = lax.dynamic_slice_in_dim(tile_lists, block_id, 1, 0)[0]
    contract_rows = (((0,), (0,)), ((), ()))
    within = jnp.arange(tile_rows, dtype=jnp.int32)
    wanted_rows = (my_tiles[:, None] * tile_rows + within[None, :]).reshape(width)
    piece = lax.all_gather(probe_block, "obs", axis=0, tiled=True)
    global_rows = jnp.arange(piece.shape[0], dtype=jnp.int32)
    selector = (wanted_rows[:, None] == global_rows[None, :]).astype(jnp.bfloat16)
    probe_cols = jnp.dot(selector, piece, preferred_element_type=jnp.float32).astype(jnp.bfloat16)
    image = jnp.dot(jacobian, probe_cols, preferred_element_type=jnp.float32).astype(jnp.bfloat16)
    partial_prod = lax.dot_general(
        weighted, image, contract_rows, preferred_element_type=jnp.float32
    )
    tile_ids = jnp.arange(tile_count, dtype=jnp.int32)
    slots = jnp.sum(
        (my_tiles[:, None] == tile_ids[None, :]).astype(jnp.int32) * tile_slot[None, :], axis=1
    )
    positions = jnp.arange(tiles_listed, dtype=jnp.int32)
    block_sum = lax.psum_scatter(partial_prod, "sub", scatter_dimension=1, tiled=True)
    targets = jnp.arange(own_rows * lax.axis_size("obs"), dtype=jnp.int32)
    target_slot = targets // tile_rows
    match = (slots[None, :] == target_slot[:, None]).astype(jnp.int32)
    found = jnp.sum(match, axis=1)
    where_at = jnp.sum(match * positions[None, :], axis=1)
    source_rows = where_at * tile_rows + targets % tile_rows
    taken = jnp.take(block_sum, source_rows, axis=0)
    summed = lax.psum_scatter(
        taken * found[:, None].astype(jnp.float32), "obs", scatter_dimension=0, tiled=True
    )
    return summed.astype(jnp.bfloat16)


def solution(mesh):
    placed = (P(("obs", "sub"), None), P(("obs", "sub")), P("obs"), P(), P(), P("obs", None))
    return jax.shard_map(
        local, mesh=mesh, in_specs=placed, out_specs=P("obs", "sub"), check_vma=False
    )
```

profile of v0, /device:TPU:8, one launch (start us, length us, event | category | flops | bytes accessed | tf_op | source)
XLA Modules:
  0.0 300.9 jit_solution(16359943806372789093)
XLA Ops:
  6.5 0.0 copy-start
  6.5 0.0 all-gather.2.cloned.1.call-start
  6.5 0.7 all-gather.2.cloned.1.call-update
  7.3 0.0 reduce-scatter.3.cloned.1.call-start
  8.0 0.0 copy-done
  8.0 0.2 dynamic-slice_reduce_fusion
  8.2 0.1 add_bitcast_fusion
  8.2 0.7 fusion.18
  8.9 81.4 %all-gather.2.cloned.1.call-done = bf16[4096,256]{1,0:T(8,128)(2,1)} async-done(((bf16[64,256]{1,0:T(8,128)(2,1)}), bf16[4096,256]{1,0:T(8,128)(2,1)}) %all-gather.2.cloned.1.call-update) | async-done | bytes 2097168 | tf_op jit(solution)/shard_map/all_gather | solution.py:24
  90.3 11.4 %fusion.6 = bf16[256,1024]{1,0:T(8,128)(2,1)S(1)} fusion(bf16[1024,2048]{1,0:T(8,128)(2,1)} %param.6, bf16[4096,256]{1,0:T(8,128)(2,1)} %all-gather.2.cloned.1.call-done, s32[2048]{0:T(1024)S(1)} %bitcast.12), kind=kOutput, calls=%fused_computation.10 | convolution fusion | flops 5377884160 | bytes 6823936 | tf_op jit(solution)/shard_map/dot_general | solution.py:28
  101.7 4.9 %fusion.2 = f32[2048,256]{0,1:T(8,128)} fusion(bf16[256,1024]{1,0:T(8,128)(2,1)S(1)} %fusion.6, bf16[1024,2048]{1,0:T(8,128)(2,1)} %param.6, f32[1024]{0:T(1024)S(1)} %fusion.18), kind=kOutput, calls=%fused_computation.5 | convolution fusion | flops 1080033280 | bytes 6819840 | tf_op jit(solution)/shard_map/dot_general | solution.py:29
  106.6 0.0 copy-start.1
  106.6 0.0 reduce-scatter.3.cloned.1.call-update
  106.7 0.0 reduce-scatter.5.cloned.1.call-start
  106.7 0.6 copy-done.1
  107.3 0.2 select_reduce_fusion
  107.5 0.1 fusion.8
  107.7 27.8 %reduce-scatter.3.cloned.1.call-done = f32[2048,64]{0,1:T(8,128)} async-done(((f32[2048,256]{0,1:T(8,128)}), f32[2048,64]{0,1:T(8,128)}) %reduce-scatter.3.cloned.1.call-update) | async-done | bytes 524304 | tf_op jit(solution)/shard_map/reduce_scatter | solution.py:37
  135.5 1.4 copy.9
  136.9 10.8 %gather_fusion = f32[4096,64]{1,0:T(8,128)S(1)} fusion(f32[2048,64]{1,0:T(8,128)S(1)} %copy.9, s32[4096]{0:T(1024)S(1)} %broadcast_clamp_fusion), kind=kCustom, calls=%fused_computation | custom fusion | bytes 2113536 | tf_op jit(solution)/shard_map/jit(_take)/gather | solution.py:44
  147.6 2.7 select_multiply_fusion
  150.3 0.0 reduce-scatter.5.cloned.1.call-update
  150.3 142.7 %reduce-scatter.5.cloned.1.call-done = f32[64,64]{1,0:T(8,128)} async-done(((f32[4096,64]{1,0:T(8,128)}), f32[64,64]{1,0:T(8,128)}) %reduce-scatter.5.cloned.1.call-update) | async-done | bytes 16400 | tf_op jit(solution)/shard_map/reduce_scatter | solution.py:45
  293.0 1.4 convert_element_type.36
  (8 shorter events, 0.1 us)
Async XLA Ops:
  6.5 1.4 copy-start
  6.5 83.8 %all-gather.2.cloned.1.call-start = ((), (), s32[]{:S(2)}) async-start(), calls=%async_computation.2 | async-start | bytes 2129920 | tf_op jit(solution)/shard_map/all_gather | solution.py:24
  7.3 128.2 %reduce-scatter.3.cloned.1.call-start = ((), (), s32[]{:S(2)}) async-start(), calls=%async_computation.3 | async-start | bytes 2621440 | tf_op jit(solution)/shard_map/reduce_scatter | solution.py:37
  106.6 0.7 copy-start.1
  106.7 186.4 %reduce-scatter.5.cloned.1.call-start = ((), (), s32[]{:S(2)}) async-start(), calls=%async_computation.4 | async-start | bytes 2129920 | tf_op jit(solution)/shard_map/reduce_scatter | solution.py:45
Sparse Core Ops, SparseCore 0:
  10.1 80.1 all-gather.1
  106.8 28.6 reduce-scatter.2
  150.4 142.5 reduce-scatter.4
where the time goes:
time: 301 us
  waiting for transfers between devices  253 us (84%)
  matrix products  16.3 us (5%)
  between operations  13.8 us (5%)
  local copies, waits for them, and re-layouts  12.9 us (4%)
  other arithmetic  5.19 us (2%)
    reduce_scatter x1, waiting for transfers between devices, local(): lax.psum_scatter(taken * found[:, None].astype(jnp.float32), 'obs', scatt...  143 us
    all_gather x1, waiting for transfers between devices, local(): piece = lax.all_gather(probe_block, 'obs', axis=0, tiled=True)  81.4 us
    reduce_scatter x1, waiting for transfers between devices, local(): lax.psum_scatter(partial_prod, 'sub', scatter_dimension=1, tiled=True)  27.8 us
    dot_general x1, matrix products, local(): jnp.dot(jacobian, probe_cols, preferred_element_type=jnp.float32)  11.4 us
    gather x1, local copies, waits for them, and re-layouts, local(): taken = jnp.take(block_sum, source_rows, axis=0)  10.8 us
  transfers between devices with their start and end apart: 3, of which 3 were waited for; matrix products, arithmetic and copies ran while one was open for 0% of the time, Pallas kernels for 0%

commit v1 on v0

--- a/solution.py
+++ b/solution.py
@@ -21,7 +21,10 @@
     contract_rows = (((0,), (0,)), ((), ()))
     within = jnp.arange(tile_rows, dtype=jnp.int32)
     wanted_rows = (my_tiles[:, None] * tile_rows + within[None, :]).reshape(width)
-    piece = lax.all_gather(probe_block, "obs", axis=0, tiled=True)
+    size = lax.axis_size("obs")
+    blocks = jnp.stack([probe_block for _ in range(size)])
+    blocks = lax.all_to_all(blocks, "obs", split_axis=0, concat_axis=0)
+    piece = jnp.concatenate(blocks, axis=0)
     global_rows = jnp.arange(piece.shape[0], dtype=jnp.int32)
     selector = (wanted_rows[:, None] == global_rows[None, :]).astype(jnp.bfloat16)
     probe_cols = jnp.dot(selector, piece, preferred_element_type=jnp.float32).astype(jnp.bfloat16)

time: 301 us -> 282 us (0.937)
  waiting for transfers between devices: 253 us -> 219 us
  starting transfers between devices: 0.08 us -> 12.1 us
    all_gather x1 -> x0, waiting for transfers between devices: 81.4 us -> none  [local(): piece = lax.all_gather(probe_block, 'obs', axis=0, tiled=True)]
    all_to_all x0 -> x1, waiting for transfers between devices: none -> 50.3 us  [local(): blocks = lax.all_to_all(blocks, 'obs', split_axis=0, concat_axis=0)]
    all_to_all x0 -> x1, starting transfers between devices: none -> 12.1 us  [local(): blocks = lax.all_to_all(blocks, 'obs', split_axis=0, concat_axis=0)]
where the time goes in v1:
time: 282 us; the launch traced here: 281 us
  waiting for transfers between devices  219 us (78%)
  matrix products  15.7 us (6%)
  local copies, waits for them, and re-layouts  15.3 us (5%)
  between operations  14.2 us (5%)
  starting transfers between devices  12.1 us (4%)
  other arithmetic  4.5 us (2%)
    reduce_scatter x1, waiting for transfers between devices, local(): lax.psum_scatter(taken * found[:, None].astype(jnp.float32), 'obs', scatt...  143 us
    all_to_all x1, waiting for transfers between devices, local(): blocks = lax.all_to_all(blocks, 'obs', split_axis=0, concat_axis=0)  50.3 us
    reduce_scatter x1, waiting for transfers between devices, local(): lax.psum_scatter(partial_prod, 'sub', scatter_dimension=1, tiled=True)  26.4 us
    all_to_all x1, starting transfers between devices, local(): blocks = lax.all_to_all(blocks, 'obs', split_axis=0, concat_axis=0)  12.1 us
    dot_general x1, matrix products, local(): jnp.dot(jacobian, probe_cols, preferred_element_type=jnp.float32)  10.8 us
    gather x1, local copies, waits for them, and re-layouts, local(): taken = jnp.take(block_sum, source_rows, axis=0)  10.8 us
  transfers between devices with their start and end apart: 3, of which 3 were waited for; matrix products, arithmetic and copies ran while one was open for 0% of the time, Pallas kernels for 0%

profile of v1, /device:TPU:8, one launch (start us, length us, event | category | flops | bytes accessed | tf_op | source)
XLA Modules:
  0.0 281.2 jit_solution(925382747368301808)
XLA Ops:
  6.5 0.0 copy-start
  6.5 2.4 stack.2
  8.9 0.0 copy-start.1
  8.9 12.1 %all-to-all-start = ((bf16[64,64,256]{2,1,0:T(8,128)(2,1)}), bf16[64,64,256]{2,1,0:T(8,128)(2,1)S(1)}, u32[]{:S(2)}, u32[]{:S(2)}) async-start(bf16[64,64,256]{2,1,0:T(8,128)(2,1)} %stack.2), calls=%async_computation | async-start | bytes 4194304 | tf_op jit(solution)/shard_map/all_to_all | solution.py:26
  21.0 0.0 reduce-scatter.3.cloned.1.call-start
  21.0 0.0 copy-done
  21.1 0.2 dynamic-slice_reduce_fusion
  21.2 0.1 add_bitcast_fusion
  22.0 0.0 copy-done.1
  22.0 50.3 %all-to-all-done = bf16[64,64,256]{2,1,0:T(8,128)(2,1)S(1)} async-done(((bf16[64,64,256]{2,1,0:T(8,128)(2,1)}), bf16[64,64,256]{2,1,0:T(8,128)(2,1)S(1)}, u32[]{:S(2)}, u32[]{:S(2)}) %all-to-all-start) | async-done | bytes 2097184 | tf_op jit(solution)/shard_map/all_to_all | solution.py:26
  72.3 10.8 %fusion.6 = bf16[256,1024]{1,0:T(8,128)(2,1)S(1)} fusion(bf16[1024,2048]{1,0:T(8,128)(2,1)} %param.6, bf16[4096,256]{1,0:T(8,128)(2,1)S(1)} %bitcast.11, s32[2048]{0:T(1024)S(1)} %bitcast.14), kind=kOutput, calls=%fused_computation.10 | convolution fusion | flops 5377884160 | bytes 6823936 | tf_op jit(solution)/shard_map/dot_general | solution.py:31
  83.1 4.9 %fusion.2 = f32[2048,256]{0,1:T(8,128)} fusion(bf16[256,1024]{1,0:T(8,128)(2,1)S(1)} %fusion.6, bf16[1024,2048]{1,0:T(8,128)(2,1)} %param.6, f32[1024]{0:T(1024)S(1)} %fusion.18), kind=kOutput, calls=%fused_computation.5 | convolution fusion | flops 1080033280 | bytes 6819840 | tf_op jit(solution)/shard_map/dot_general | solution.py:32
  88.0 0.0 copy-start.2
  88.0 0.0 reduce-scatter.3.cloned.1.call-update
  88.1 0.0 reduce-scatter.5.cloned.1.call-start
  88.1 0.6 copy-done.2
  88.7 0.2 select_reduce_fusion
  88.9 0.1 fusion.8
  89.1 26.4 %reduce-scatter.3.cloned.1.call-done = f32[2048,64]{0,1:T(8,128)} async-done(((f32[2048,256]{0,1:T(8,128)}), f32[2048,64]{0,1:T(8,128)}) %reduce-scatter.3.cloned.1.call-update) | async-done | bytes 524304 | tf_op jit(solution)/shard_map/reduce_scatter | solution.py:40
  115.5 1.4 copy.9
  116.9 10.8 %gather_fusion = f32[4096,64]{1,0:T(8,128)S(1)} fusion(f32[2048,64]{1,0:T(8,128)S(1)} %copy.9, s32[4096]{0:T(1024)S(1)} %broadcast_clamp_fusion), kind=kCustom, calls=%fused_computation | custom fusion | bytes 2113536 | tf_op jit(solution)/shard_map/jit(_take)/gather | solution.py:47
  127.7 2.7 select_multiply_fusion
  130.3 0.0 reduce-scatter.5.cloned.1.call-update
  130.3 142.6 %reduce-scatter.5.cloned.1.call-done = f32[64,64]{1,0:T(8,128)} async-done(((f32[4096,64]{1,0:T(8,128)}), f32[64,64]{1,0:T(8,128)}) %reduce-scatter.5.cloned.1.call-update) | async-done | bytes 16400 | tf_op jit(solution)/shard_map/reduce_scatter | solution.py:48
  273.0 1.4 convert_element_type.36
  (9 shorter events, 0.1 us)
Async XLA Ops:
  6.5 14.5 %copy-start = (s32[64,8]{0,1:T(8,128)S(1)}, s32[64,8]{0,1:T(8,128)}, u32[]{:S(2)}) copy-start(s32[64,8]{0,1:T(8,128)} %param.9) | copy-start | bytes 6148
  8.9 13.1 %copy-start.1 = (f32[1024]{0:T(1024)S(1)}, f32[1024]{0:T(1024)}, u32[]{:S(2)}) copy-start(f32[1024]{0:T(1024)} %param.7) | copy-start | bytes 12292
  8.9 63.4 %all-to-all-start = ((bf16[64,64,256]{2,1,0:T(8,128)(2,1)}), bf16[64,64,256]{2,1,0:T(8,128)(2,1)S(1)}, u32[]{:S(2)}, u32[]{:S(2)}) async-start(bf16[64,64,256]{2,1,0:T(8,128)(2,1)} %stack.2), calls=%async_computation | async-start | bytes 4194304 | tf_op jit(solution)/shard_map/all_to_all | solution.py:26
  21.0 94.5 %reduce-scatter.3.cloned.1.call-start = ((), (), s32[]{:S(2)}) async-start(), calls=%async_computation.3 | async-start | bytes 2621440 | tf_op jit(solution)/shard_map/reduce_scatter | solution.py:40
  88.0 0.7 copy-start.2
  88.1 184.9 %reduce-scatter.5.cloned.1.call-start = ((), (), s32[]{:S(2)}) async-start(), calls=%async_computation.4 | async-start | bytes 2129920 | tf_op jit(solution)/shard_map/reduce_scatter | solution.py:48
Sparse Core Ops, SparseCore 0:
  88.2 27.2 reduce-scatter.2
  130.5 142.4 reduce-scatter.4
